TPU v7x, 256 devices: a whole 4x4x8 slice. The times are simulated.
256 devices in a mesh: layer: 4 (over y), row: 8 (over x, core), col: 8 (over z).
Axes of the slice: x: 4, y: 4, z: 8, core: 2. Of those that a mesh axis runs over, the one named last changes fastest.
Arguments:
- l_blocks: bfloat16 [4, 64, 256, 256], P('layer', ('row', 'col')), may hold values from -3 to 3
- l_ids: int32 [4, 64], P('layer'), may hold values from 0 to 127, as said below
- u_blocks: bfloat16 [4, 64, 256, 256], P('layer', ('row', 'col')), may hold values from -3 to 3
- u_ids: int32 [4, 64], P('layer'), may hold values from 0 to 127, as said below
- inv_upper: bfloat16 [8, 256, 256], replicated, as said below
- inv_lower: bfloat16 [8, 256, 256], replicated, as said below
- row_order: int32 [16], replicated, may hold values from 0 to 15, as said below
- col_order: int32 [16], replicated, may hold values from 0 to 15, as said below
- front_in: float32 [16, 16, 256, 256], P('row', 'col', 'layer'), may hold values from -6 to 6
- leaf_lower: bfloat16 [256, 1024, 1024], P(('layer', 'row', 'col')), may hold values from -6 to 6
- leaf_upper: bfloat16 [256, 1024, 1024], P(('layer', 'row', 'col')), may hold values from -0.1875 to 0.1875
- leaf_front: bfloat16 [256, 1024, 1024], P(('layer', 'row', 'col')), may hold values from -6 to 6
Outputs:
- front_out: float32 [16, 16, 256, 256], P('row', 'col', 'layer')
- leaf_out: bfloat16 [256, 1024, 1024], P(('layer', 'row', 'col'))
Inputs may be any that keep to these rules, and one draw needn't show every extreme that they name: `l_ids`: within a layer the ids are distinct; the entry at index r * 8 + c has i = row_order[r * 2 + p] for some p < 2. `u_ids`: within a layer the ids are distinct; the entry at index r * 8 + c has j = col_order[c * 2 + q] for some q < 2. `row_order`: A permutation of the tile rows. `col_order`: A permutation of the tile columns. `inv_upper`: each block is upper triangular with a positive diagonal. `inv_lower`: each block is lower triangular with a positive diagonal.
All inputs are finite; a program needn't handle non-finite values.
Results may differ from a plain program's by a relative error of at most 0.0095.
Values may be sent and summed in bfloat16 or wider, within the bound.
No kernel may reach another device: no remote copies, remote signals or barrier semaphores. Data moves between devices by JAX's collectives and lax.ppermute only.
A program may use at most 128 MiB of HBM per device.

v0:
```python
import functools

import jax
import jax.numpy as jnp
from jax import lax
from jax.experimental import pallas as pl
from jax.experimental.pallas import tpu as pltpu
from jax.sharding import PartitionSpec as P


U_FLIPS = (0, 2, 6, 4, 1, 3, 7, 5)
L_STEPS = ((0, 0), (0, 1), (0, -1), (4, 0), (4, 1), (4, -1), (0, 2), (0, -2))
COLS = 8
BLOCKS = 64
TILES = 16
VMEM_LIMIT = 16 << 20
VMEM = pl.BlockSpec(memory_space=pltpu.VMEM)
SMEM = pl.BlockSpec(memory_space=pltpu.SMEM)


def swap_with(x, axis, size, partner):
    return lax.ppermute(x, axis, [(i, partner(i) % size) for i in range(size)])


def other_pair(i):
    return i + 1 if i % 2 else i - 1


def call(body, outs, ins, args, flops, moved, scratch=(), out_specs=None):
    return pl.pallas_call(
        body,
        out_shape=outs,
        in_specs=ins,
        out_specs=out_specs or jax.tree.map(lambda _: VMEM, outs),
        scratch_shapes=list(scratch),
        cost_estimate=pl.CostEstimate(flops=flops, bytes_accessed=moved, transcendentals=0),
        compiler_params=pltpu.CompilerParams(vmem_limit_bytes=VMEM_LIMIT),
    )(*args)


def add_upper(block, n, meta, inv, up):
    r = lax.axis_index("row")
    c = lax.axis_index("col")
    tile = inv.shape[-1]
    ident = meta[0, (r ^ U_FLIPS[n]) * COLS + c]
    k = lax.div(ident, TILES)
    q = jnp.where(lax.rem(ident, TILES) == meta[0, 2 * BLOCKS + 2 * c + 1], 1, 0)
    prod = jnp.dot(inv[k], block, preferred_element_type=jnp.float32).astype(jnp.bfloat16)
    up[k, :, pl.ds(pl.multiple_of(q * tile, tile), tile)] = prod


def add_lower(block, n, meta, inv, up, acc):
    r = lax.axis_index("row")
    c = lax.axis_index("col")
    panels = up.shape[0]
    whole, sided = L_STEPS[n]
    step = whole + sided * (1 - 2 * lax.rem(c, 2))
    ident = meta[0, BLOCKS + r * COLS + lax.rem(c + step + COLS, COLS)]
    k = lax.rem(ident, panels)
    p = jnp.where(lax.div(ident, panels) == meta[0, 2 * BLOCKS + TILES + 2 * r + 1], 1, 0)
    low = jnp.dot(block, inv[panels + k], preferred_element_type=jnp.float32).astype(jnp.bfloat16)
    acc[p] += jnp.dot(low, up[k], preferred_element_type=jnp.float32)


def near_body(meta, inv, *refs):
    uppers, lowers, (up, acc) = refs[: len(U_FLIPS)], refs[len(U_FLIPS) : -2], refs[-2:]
    up[...] = jnp.zeros_like(up)
    acc[...] = jnp.zeros_like(acc)
    for n, ref in enumerate(uppers):
        add_upper(ref[...], n, meta, inv, up)
    for n, ref in enumerate(lowers):
        add_lower(ref[...], n, meta, inv, up, acc)


def mid_body(meta, inv, up, acc_in, *refs, first):
    acc = refs[-1]
    acc[...] = acc_in[...]
    for n, ref in enumerate(refs[:-1]):
        add_lower(ref[...], first + n, meta, inv, up, acc)


def far_body(meta, inv, up, acc_in, *refs, first):
    lowers, (s1, s2, s3, own, acc) = refs[:-5], refs[-5:]
    acc[...] = acc_in[...]
    for n, ref in enumerate(lowers):
        add_lower(ref[...], first + n, meta, inv, up, acc)
    layer = lax.axis_index("layer")
    part, tile = own.shape[2:]
    for flip, dst in ((2, s2), (1, s1), (3, s3), (0, own)):
        at = pl.multiple_of((layer ^ flip) * part, part)
        for p in range(2):
            for q in range(2):
                dst[p, q] = acc[p, pl.ds(at, part), q * tile : (q + 1) * tile].astype(dst.dtype)


def program(
    l_blocks,
    l_ids,
    u_blocks,
    u_ids,
    inv_upper,
    inv_lower,
    row_order,
    col_order,
    front_in,
    leaf_lower,
    leaf_upper,
    leaf_front,
):
    tile = l_blocks.shape[-1]
    panels = inv_upper.shape[0]
    part = front_in.shape[2]
    rows = lax.axis_size("row")
    cols = lax.axis_size("col")
    layers = lax.axis_size("layer")
    bf, f32 = jnp.bfloat16, jnp.float32
    sds = jax.ShapeDtypeStruct

    b = l_blocks[0, 0]
    u = u_blocks[0, 0]
    b4 = swap_with(b, "col", cols, lambda i: i + cols // 2)
    be = swap_with(b, "col", cols, lambda i: i ^ 1)
    bo = swap_with(b, "col", cols, other_pair)
    ue = swap_with(u, "row", rows, lambda i: i ^ 2)
    uo = swap_with(u, "row", rows, lambda i: i ^ 6)
    u2 = swap_with(u, "row", rows, lambda i: i ^ 4)
    ours = (u, ue, uo, u2)
    fe = swap_with(bo, "col", cols, lambda i: i ^ 1)
    fo = swap_with(be, "col", cols, other_pair)
    ge = swap_with(b4, "col", cols, lambda i: i ^ 1)
    go = swap_with(b4, "col", cols, other_pair)
    near, mid, far = (b, be, bo, b4), (), (ge, go, fe, fo)
    theirs = tuple(swap_with(x, "row", rows, lambda i: i ^ 1) for x in ours)
    meta = jnp.concatenate([u_ids, l_ids, col_order[None], row_order[None]], axis=1)
    invs = jnp.concatenate([inv_lower, inv_upper])

    up, acc = call(
        near_body,
        (sds((panels, tile, 2 * tile), bf), sds((2, tile, 2 * tile), f32)),
        [SMEM] + [VMEM] * (1 + 8 + len(near)),
        (meta, invs, *ours, *theirs, *near),
        flops=2 * (8 + 3 * len(near)) * tile**3,
        moved=4 << 20,
    )
    if mid:
        acc = call(
            functools.partial(mid_body, first=len(near)),
            sds((2, tile, 2 * tile), f32),
            [SMEM] + [VMEM] * (3 + len(mid)),
            (meta, invs, up, acc, *mid),
            flops=2 * 3 * len(mid) * tile**3,
            moved=4 << 20,
        )
    piece = (2, 2, part, tile)
    s1, s2, s3, own = call(
        functools.partial(far_body, first=len(near) + len(mid)),
        (sds(piece, bf), sds(piece, bf), sds(piece, bf), sds(piece, f32)),
        [SMEM] + [VMEM] * (3 + len(far)),
        (meta, invs, up, acc, *far),
        flops=2 * 3 * len(far) * tile**3,
        moved=4 << 20,
        scratch=[pltpu.VMEM((2, tile, 2 * tile), f32)],
    )
    r2 = swap_with(s2, "layer", layers, lambda i: i ^ 2)
    r1 = swap_with(s1, "layer", layers, lambda i: i ^ 1)
    r3 = swap_with(s3, "layer", layers, lambda i: i ^ 3)
    front_out = front_in - (own + r1.astype(f32) + r2.astype(f32) + r3.astype(f32))

    update = jnp.dot(leaf_lower[0], leaf_upper[0], preferred_element_type=f32)
    leaf_out = (leaf_front[0].astype(f32) - update).astype(bf)[None]
    return (front_out, leaf_out)


def solution(mesh):
    return jax.shard_map(
        program,
        mesh=mesh,
        in_specs=(
            P("layer", ("row", "col"), None, None),
            P("layer", None),
            P("layer", ("row", "col"), None, None),
            P("layer", None),
            P(),
            P(),
            P(),
            P(),
            P("row", "col", "layer", None),
            P(("layer", "row", "col"), None, None),
            P(("layer", "row", "col"), None, None),
            P(("layer", "row", "col"), None, None),
        ),
        out_specs=(P("row", "col", "layer", None), P(("layer", "row", "col"), None, None)),
        check_vma=False,
    )
```

profile of v0, /device:TPU:2, one launch (start us, length us, event | category | flops | bytes accessed | tf_op | source)
XLA Modules:
  0.0 45.3 jit_solution(12584350092984823860)
XLA Ops:
  0.6 0.0 copy-start
  0.6 0.0 copy-start.2
  0.7 0.0 copy-start.3
  0.7 2.3 %collective-permute-start = (bf16[256,256]{1,0:T(8,128)(2,1)}, bf16[256,256]{1,0:T(8,128)(2,1)S(1)}, u32[]{:S(2)}, u32[]{:S(2)}) collective-permute-start(bf16[256,256]{1,0:T(8,128)(2,1)} %bitcast.19), channel_id=1, source_target_pairs={{0,16},{8,24},{16,0},{24,8},{32,48},{40,56},{48,32},{56,40},{1,17}... | collective-permute-start | bytes 393224 | tf_op jit(solution)/shard_map/ppermute | solution.py:22
  3.0 0.4 collective-permute-start.1
  3.4 1.7 %collective-permute-start.2 = (bf16[256,256]{1,0:T(8,128)(2,1)}, bf16[256,256]{1,0:T(8,128)(2,1)S(1)}, u32[]{:S(2)}, u32[]{:S(2)}) collective-permute-start(bf16[256,256]{1,0:T(8,128)(2,1)} %bitcast.21), channel_id=1, source_target_pairs={{0,32},{8,40},{16,48},{24,56},{32,0},{40,8},{48,16},{56,24},{1,33}... | collective-permute-start | bytes 393224 | tf_op jit(solution)/shard_map/ppermute | solution.py:22
  5.2 0.0 collective-permute-start.3
  5.2 0.0 copy-start.5
  5.2 0.0 copy-start.6
  5.2 0.0 copy-start.7
  5.2 0.0 copy-start.8
  5.2 0.0 copy-start.1
  5.2 7.0 %collective-permute-start.9 = (bf16[256,256]{1,0:T(8,128)(2,1)}, bf16[256,256]{1,0:T(8,128)(2,1)S(1)}, u32[]{:S(2)}, u32[]{:S(2)}) collective-permute-start(bf16[256,256]{1,0:T(8,128)(2,1)} %bitcast.24), channel_id=1, source_target_pairs={{0,4},{1,5},{2,6},{3,7},{4,0},{5,1},{6,2},{7,3},{8,12},{9,13},{10,... | collective-permute-start | bytes 393224 | tf_op jit(solution)/shard_map/ppermute | solution.py:22
  12.2 1.3 %constant_dynamic-update-slice_fusion.1 = bf16[16,256,256]{2,1,0:T(8,128)(2,1)S(1)} fusion(bf16[8,256,256]{2,1,0:T(8,128)(2,1)} %param.17), kind=kLoop, calls=%fused_computation.8 | loop fusion | bytes 2097152
  13.5 0.0 collective-permute-done.refs_1_
  13.5 0.0 copy-done.2
  13.5 1.1 %collective-permute-start.7 = (bf16[256,256]{1,0:T(8,128)(2,1)S(1)}, bf16[256,256]{1,0:T(8,128)(2,1)S(1)}, u32[]{:S(2)}, u32[]{:S(2)}) collective-permute-start(bf16[256,256]{1,0:T(8,128)(2,1)S(1)} %bitcast.25), channel_id=1, source_target_pairs={{0,1},{1,0},{2,3},{3,2},{4,5},{5,4},{6,7},{7,6},{8,9},{9,8},{10,11... | collective-permute-start | bytes 393224 | tf_op jit(solution)/shard_map/ppermute | solution.py:22
  14.6 0.0 collective-permute-done.1.refs_2_
  14.6 0.3 collective-permute-start.8
  14.9 0.0 collective-permute-done.2.refs_3_
  14.9 0.0 collective-permute-start.4
  14.9 3.2 %collective-permute-done.9.refs_11_ = bf16[256,256]{1,0:T(8,128)(2,1)S(1)} collective-permute-done((bf16[256,256]{1,0:T(8,128)(2,1)}, bf16[256,256]{1,0:T(8,128)(2,1)S(1)}, u32[]{:S(2)}, u32[]{:S(2)}) %collective-permute-start.9) | collective-permute-done | bytes 131104 | tf_op jit(solution)/shard_map/ppermute | solution.py:22
  18.1 0.0 collective-permute-start.5
  18.1 0.0 collective-permute-done.3.refs_4_
  18.1 0.5 %collective-permute-start.6 = (bf16[256,256]{1,0:T(8,128)(2,1)S(1)}, bf16[256,256]{1,0:T(8,128)(2,1)S(1)}, u32[]{:S(2)}, u32[]{:S(2)}) collective-permute-start(bf16[256,256]{1,0:T(8,128)(2,1)S(1)} %collective-permute-done.2.refs_3_), channel_id=1, source_target_pairs={{0,8},{8,0},{16,24},{24,16},{32,40},{40,32},{48,56},{56,48},{1,9},... | collective-permute-start | bytes 393224 | tf_op jit(solution)/shard_map/ppermute | solution.py:22
  18.6 0.0 copy-done.3
  18.6 0.1 constant_dynamic-update-slice_fusion.inv
  18.7 4.2 %collective-permute-done.7.refs_9_ = bf16[256,256]{1,0:T(8,128)(2,1)S(1)} collective-permute-done((bf16[256,256]{1,0:T(8,128)(2,1)S(1)}, bf16[256,256]{1,0:T(8,128)(2,1)S(1)}, u32[]{:S(2)}, u32[]{:S(2)}) %collective-permute-start.7) | collective-permute-done | bytes 131104 | tf_op jit(solution)/shard_map/ppermute | solution.py:22
  22.9 0.2 collective-permute-start.10
  23.2 0.0 collective-permute-done.8.refs_10_
  23.2 2.6 %collective-permute-start.11 = (bf16[256,256]{1,0:T(8,128)(2,1)S(1)}, bf16[256,256]{1,0:T(8,128)(2,1)S(1)}, u32[]{:S(2)}, u32[]{:S(2)}) collective-permute-start(bf16[256,256]{1,0:T(8,128)(2,1)S(1)} %collective-permute-done.9.refs_11_), channel_id=1, source_target_pairs={{0,7},{1,2},{2,1},{3,4},{4,3},{5,6},{6,5},{7,0},{8,15},{9,10},{10,... | collective-permute-start | bytes 393224 | tf_op jit(solution)/shard_map/ppermute | solution.py:22
  25.8 0.0 collective-permute-done.4.refs_5_
  25.8 0.2 collective-permute-start.12
  26.0 0.0 collective-permute-done.5.refs_6_
  26.0 1.1 %collective-permute-start.13 = (bf16[256,256]{1,0:T(8,128)(2,1)S(1)}, bf16[256,256]{1,0:T(8,128)(2,1)S(1)}, u32[]{:S(2)}, u32[]{:S(2)}) collective-permute-start(bf16[256,256]{1,0:T(8,128)(2,1)S(1)} %collective-permute-done.7.refs_9_), channel_id=1, source_target_pairs={{0,7},{1,2},{2,1},{3,4},{4,3},{5,6},{6,5},{7,0},{8,15},{9,10},{10,... | collective-permute-start | bytes 393224 | tf_op jit(solution)/shard_map/ppermute | solution.py:22
  27.1 0.0 copy-done.5
  27.1 0.0 copy-done.6
  27.1 0.0 copy-done.7
  27.1 0.0 copy-done.8
  27.1 0.1 pad_add_fusion.meta
  27.2 0.0 collective-permute-done.6.refs_7_
  27.2 0.0 copy-done.1
  27.2 1.9 %shard_map.131 = (bf16[8,256,512]{2,1,0:T(8,128)(2,1)S(1)}, f32[2,256,512]{2,1,0:T(8,128)S(1)}) custom-call(s32[1,160]{1,0:T(1,128)S(1)} %pad_add_fusion.meta, bf16[16,256,256]{2,1,0:T(8,128)(2,1)S(1)} %constant_dynamic-update-slice_fusion.inv, bf16[256,256]{1,0:T(8,128)(2,1)S(1)} %bitcast.23, bf16[256,256]{1,0:T(8,128)(2,1)S(1)} %collective-permute-done.refs_1_, ...), custom_call_target="tpu_custom_call" | custom-call | flops 671088640 | bytes 4194304 | tf_op jit(solution)/shard_map/pallas_call | solution.py:30
  29.2 0.0 collective-permute-done.10.refs_0_
  29.2 0.5 %collective-permute-done.11.refs_1_ = bf16[256,256]{1,0:T(8,128)(2,1)S(1)} collective-permute-done((bf16[256,256]{1,0:T(8,128)(2,1)S(1)}, bf16[256,256]{1,0:T(8,128)(2,1)S(1)}, u32[]{:S(2)}, u32[]{:S(2)}) %collective-permute-start.11) | collective-permute-done | bytes 131104 | tf_op jit(solution)/shard_map/ppermute | solution.py:22
  29.7 1.1 %collective-permute-done.12.refs_2_ = bf16[256,256]{1,0:T(8,128)(2,1)S(1)} collective-permute-done((bf16[256,256]{1,0:T(8,128)(2,1)S(1)}, bf16[256,256]{1,0:T(8,128)(2,1)S(1)}, u32[]{:S(2)}, u32[]{:S(2)}) %collective-permute-start.12) | collective-permute-done | bytes 131104 | tf_op jit(solution)/shard_map/ppermute | solution.py:22
  30.8 1.4 %collective-permute-done.13.refs_3_ = bf16[256,256]{1,0:T(8,128)(2,1)S(1)} collective-permute-done((bf16[256,256]{1,0:T(8,128)(2,1)S(1)}, bf16[256,256]{1,0:T(8,128)(2,1)S(1)}, u32[]{:S(2)}, u32[]{:S(2)}) %collective-permute-start.13) | collective-permute-done | bytes 131104 | tf_op jit(solution)/shard_map/ppermute | solution.py:22
  32.2 0.0 copy-start.9
  32.2 0.0 copy-start.10
  32.2 1.6 %shard_map.132 = (bf16[2,2,64,256]{3,2,1,0:T(8,128)(2,1)S(1)}, bf16[2,2,64,256]{3,2,1,0:T(8,128)(2,1)S(1)}, bf16[2,2,64,256]{3,2,1,0:T(8,128)(2,1)S(1)}, f32[2,2,64,256]{3,2,1,0:T(8,128)S(1)}) custom-call(s32[1,160]{1,0:T(1,128)S(1)} %pad_add_fusion.meta, bf16[16,256,256]{2,1,0:T(8,128)(2,1)S(1)} %constant_dynamic-update-slice_fusion.inv, ...), custom_call_target="tpu_custom_call" | custom-call | flops 402653184 | bytes 4194304 | tf_op jit(solution)/shard_map/pallas_call | solution.py:30
  33.8 1.7 %collective-permute-start.14 = (bf16[2,2,64,256]{3,2,1,0:T(8,128)(2,1)S(1)}, bf16[2,2,64,256]{3,2,1,0:T(8,128)(2,1)S(1)}, u32[]{:S(2)}, u32[]{:S(2)}) collective-permute-start(bf16[2,2,64,256]{3,2,1,0:T(8,128)(2,1)S(1)} %get-tuple-element.11), channel_id=1, source_target_pairs={{0,64},{64,0},{128,192},{192,128},{1,65},{65,1},{129,193},{193,129... | collective-permute-start | bytes 393224 | tf_op jit(solution)/shard_map/ppermute | solution.py:22
  35.5 2.9 %collective-permute-start.15 = (bf16[2,2,64,256]{3,2,1,0:T(8,128)(2,1)S(1)}, bf16[2,2,64,256]{3,2,1,0:T(8,128)(2,1)S(1)}, u32[]{:S(2)}, u32[]{:S(2)}) collective-permute-start(bf16[2,2,64,256]{3,2,1,0:T(8,128)(2,1)S(1)} %get-tuple-element.12), channel_id=1, source_target_pairs={{0,128},{64,192},{128,0},{192,64},{1,129},{65,193},{129,1},{193,65... | collective-permute-start | bytes 393224 | tf_op jit(solution)/shard_map/ppermute | solution.py:22
  38.4 0.0 copy-start.4
  38.4 0.2 collective-permute-start.16
  38.6 0.0 copy-done
  38.6 0.0 copy-done.9
  38.6 0.0 copy-done.10
  38.6 3.7 %fusion.1 = bf16[1,1024,1024]{2,1,0:T(8,128)(2,1)} fusion(bf16[1,1024,1024]{2,1,0:T(8,128)(2,1)S(1)} %copy-done.9, bf16[1,1024,1024]{2,1,0:T(8,128)(2,1)S(1)} %copy-done, bf16[1,1024,1024]{2,1,0:T(8,128)(2,1)S(1)} %copy-done.10), kind=kOutput, calls=%fused_computation.2 | convolution fusion | flops 2150629376 | bytes 8388608 | tf_op jit(solution)/shard_map/dot_general | solution.py:169
  42.3 0.0 collective-permute-done.14
  42.3 0.7 %collective-permute-done.15 = bf16[2,2,64,256]{3,2,1,0:T(8,128)(2,1)S(1)} collective-permute-done((bf16[2,2,64,256]{3,2,1,0:T(8,128)(2,1)S(1)}, bf16[2,2,64,256]{3,2,1,0:T(8,128)(2,1)S(1)}, u32[]{:S(2)}, u32[]{:S(2)}) %collective-permute-start.15) | collective-permute-done | bytes 131104 | tf_op jit(solution)/shard_map/ppermute | solution.py:22
  43.0 1.5 %collective-permute-done.16 = bf16[2,2,64,256]{3,2,1,0:T(8,128)(2,1)S(1)} collective-permute-done((bf16[2,2,64,256]{3,2,1,0:T(8,128)(2,1)S(1)}, bf16[2,2,64,256]{3,2,1,0:T(8,128)(2,1)S(1)}, u32[]{:S(2)}, u32[]{:S(2)}) %collective-permute-start.16) | collective-permute-done | bytes 131104 | tf_op jit(solution)/shard_map/ppermute | solution.py:22
  44.5 0.0 copy-done.4
  44.5 0.8 %add_subtract_fusion = f32[2,2,64,256]{3,2,1,0:T(8,128)} fusion(f32[2,2,64,256]{3,2,1,0:T(8,128)S(1)} %copy-done.4, bf16[2,2,64,256]{3,2,1,0:T(8,128)(2,1)S(1)} %collective-permute-done.16, bf16[2,2,64,256]{3,2,1,0:T(8,128)(2,1)S(1)} %collective-permute-done.15, f32[2,2,64,256]{3,2,1,0:T(8,128)S(1)} %get-tuple-element.10, ...), kind=kLoop, calls=%fused_computation.6 | loop fusion | flops 458752 | bytes 1179648 | tf_op jit(solution)/shard_map/sub | solution.py:167
Async XLA Ops:
  0.6 38.0 %copy-start = (bf16[1,1024,1024]{2,1,0:T(8,128)(2,1)S(1)}, bf16[1,1024,1024]{2,1,0:T(8,128)(2,1)}, u32[]{:S(2)}) copy-start(bf16[1,1024,1024]{2,1,0:T(8,128)(2,1)} %param.22) | copy-start | bytes 6291460
  0.6 12.8 %copy-start.2 = (bf16[1,1,256,256]{3,2,1,0:T(8,128)(2,1)S(1)}, bf16[1,1,256,256]{3,2,1,0:T(8,128)(2,1)}, u32[]{:S(2)}) copy-start(bf16[1,1,256,256]{3,2,1,0:T(8,128)(2,1)} %param.12) | copy-start | bytes 393220
  0.7 18.0 %copy-start.3 = (bf16[8,256,256]{2,1,0:T(8,128)(2,1)S(1)}, bf16[8,256,256]{2,1,0:T(8,128)(2,1)}, u32[]{:S(2)}) copy-start(bf16[8,256,256]{2,1,0:T(8,128)(2,1)} %param.16) | copy-start | bytes 3145732
  0.7 12.8 %collective-permute-start = (bf16[256,256]{1,0:T(8,128)(2,1)}, bf16[256,256]{1,0:T(8,128)(2,1)S(1)}, u32[]{:S(2)}, u32[]{:S(2)}) collective-permute-start(bf16[256,256]{1,0:T(8,128)(2,1)} %bitcast.19), channel_id=1, source_target_pairs={{0,16},{8,24},{16,0},{24,8},{32,48},{40,56},{48,32},{56,40},{1,17}... | collective-permute-start | bytes 393224 | tf_op jit(solution)/shard_map/ppermute | solution.py:22
  3.0 11.6 %collective-permute-start.1 = (bf16[256,256]{1,0:T(8,128)(2,1)}, bf16[256,256]{1,0:T(8,128)(2,1)S(1)}, u32[]{:S(2)}, u32[]{:S(2)}) collective-permute-start(bf16[256,256]{1,0:T(8,128)(2,1)} %bitcast.20), channel_id=1, source_target_pairs={{0,48},{8,56},{16,32},{24,40},{32,16},{40,24},{48,0},{56,8},{1,49}... | collective-permute-start | bytes 393224 | tf_op jit(solution)/shard_map/ppermute | solution.py:22
  3.4 11.5 %collective-permute-start.2 = (bf16[256,256]{1,0:T(8,128)(2,1)}, bf16[256,256]{1,0:T(8,128)(2,1)S(1)}, u32[]{:S(2)}, u32[]{:S(2)}) collective-permute-start(bf16[256,256]{1,0:T(8,128)(2,1)} %bitcast.21), channel_id=1, source_target_pairs={{0,32},{8,40},{16,48},{24,56},{32,0},{40,8},{48,16},{56,24},{1,33}... | collective-permute-start | bytes 393224 | tf_op jit(solution)/shard_map/ppermute | solution.py:22
  5.2 12.9 %collective-permute-start.3 = (bf16[256,256]{1,0:T(8,128)(2,1)}, bf16[256,256]{1,0:T(8,128)(2,1)S(1)}, u32[]{:S(2)}, u32[]{:S(2)}) collective-permute-start(bf16[256,256]{1,0:T(8,128)(2,1)} %bitcast.22), channel_id=1, source_target_pairs={{0,8},{8,0},{16,24},{24,16},{32,40},{40,32},{48,56},{56,48},{1,9},... | collective-permute-start | bytes 393224 | tf_op jit(solution)/shard_map/ppermute | solution.py:22
  5.2 21.9 %copy-start.5 = (s32[16]{0:T(128)S(1)}, s32[16]{0:T(128)}, u32[]{:S(2)}) copy-start(s32[16]{0:T(128)} %param.18) | copy-start | bytes 196
  5.2 21.9 %copy-start.6 = (s32[16]{0:T(128)S(1)}, s32[16]{0:T(128)}, u32[]{:S(2)}) copy-start(s32[16]{0:T(128)} %param.19) | copy-start | bytes 196
  5.2 21.9 %copy-start.7 = (s32[1,64]{1,0:T(1,128)S(1)}, s32[1,64]{1,0:T(1,128)}, u32[]{:S(2)}) copy-start(s32[1,64]{1,0:T(1,128)} %param.13) | copy-start | bytes 772
  5.2 21.9 %copy-start.8 = (s32[1,64]{1,0:T(1,128)S(1)}, s32[1,64]{1,0:T(1,128)}, u32[]{:S(2)}) copy-start(s32[1,64]{1,0:T(1,128)} %param.15) | copy-start | bytes 772
  5.2 22.0 %copy-start.1 = (bf16[1,1,256,256]{3,2,1,0:T(8,128)(2,1)S(1)}, bf16[1,1,256,256]{3,2,1,0:T(8,128)(2,1)}, u32[]{:S(2)}) copy-start(bf16[1,1,256,256]{3,2,1,0:T(8,128)(2,1)} %param.14) | copy-start | bytes 393220
  5.2 12.9 %collective-permute-start.9 = (bf16[256,256]{1,0:T(8,128)(2,1)}, bf16[256,256]{1,0:T(8,128)(2,1)S(1)}, u32[]{:S(2)}, u32[]{:S(2)}) collective-permute-start(bf16[256,256]{1,0:T(8,128)(2,1)} %bitcast.24), channel_id=1, source_target_pairs={{0,4},{1,5},{2,6},{3,7},{4,0},{5,1},{6,2},{7,3},{8,12},{9,13},{10,... | collective-permute-start | bytes 393224 | tf_op jit(solution)/shard_map/ppermute | solution.py:22
  13.5 9.4 %collective-permute-start.7 = (bf16[256,256]{1,0:T(8,128)(2,1)S(1)}, bf16[256,256]{1,0:T(8,128)(2,1)S(1)}, u32[]{:S(2)}, u32[]{:S(2)}) collective-permute-start(bf16[256,256]{1,0:T(8,128)(2,1)S(1)} %bitcast.25), channel_id=1, source_target_pairs={{0,1},{1,0},{2,3},{3,2},{4,5},{5,4},{6,7},{7,6},{8,9},{9,8},{10,11... | collective-permute-start | bytes 393224 | tf_op jit(solution)/shard_map/ppermute | solution.py:22
  14.6 8.6 %collective-permute-start.8 = (bf16[256,256]{1,0:T(8,128)(2,1)S(1)}, bf16[256,256]{1,0:T(8,128)(2,1)S(1)}, u32[]{:S(2)}, u32[]{:S(2)}) collective-permute-start(bf16[256,256]{1,0:T(8,128)(2,1)S(1)} %bitcast.26), channel_id=1, source_target_pairs={{0,7},{1,2},{2,1},{3,4},{4,3},{5,6},{6,5},{7,0},{8,15},{9,10},{10,... | collective-permute-start | bytes 393224 | tf_op jit(solution)/shard_map/ppermute | solution.py:22
  14.9 10.9 %collective-permute-start.4 = (bf16[256,256]{1,0:T(8,128)(2,1)S(1)}, bf16[256,256]{1,0:T(8,128)(2,1)S(1)}, u32[]{:S(2)}, u32[]{:S(2)}) collective-permute-start(bf16[256,256]{1,0:T(8,128)(2,1)S(1)} %collective-permute-done.refs_1_), channel_id=1, source_target_pairs={{0,8},{8,0},{16,24},{24,16},{32,40},{40,32},{48,56},{56,48},{1,9},... | collective-permute-start | bytes 393224 | tf_op jit(solution)/shard_map/ppermute | solution.py:22
  18.1 7.9 %collective-permute-start.5 = (bf16[256,256]{1,0:T(8,128)(2,1)S(1)}, bf16[256,256]{1,0:T(8,128)(2,1)S(1)}, u32[]{:S(2)}, u32[]{:S(2)}) collective-permute-start(bf16[256,256]{1,0:T(8,128)(2,1)S(1)} %collective-permute-done.1.refs_2_), channel_id=1, source_target_pairs={{0,8},{8,0},{16,24},{24,16},{32,40},{40,32},{48,56},{56,48},{1,9},... | collective-permute-start | bytes 393224 | tf_op jit(solution)/shard_map/ppermute | solution.py:22
  18.1 9.1 %collective-permute-start.6 = (bf16[256,256]{1,0:T(8,128)(2,1)S(1)}, bf16[256,256]{1,0:T(8,128)(2,1)S(1)}, u32[]{:S(2)}, u32[]{:S(2)}) collective-permute-start(bf16[256,256]{1,0:T(8,128)(2,1)S(1)} %collective-permute-done.2.refs_3_), channel_id=1, source_target_pairs={{0,8},{8,0},{16,24},{24,16},{32,40},{40,32},{48,56},{56,48},{1,9},... | collective-permute-start | bytes 393224 | tf_op jit(solution)/shard_map/ppermute | solution.py:22
  22.9 6.2 %collective-permute-start.10 = (bf16[256,256]{1,0:T(8,128)(2,1)S(1)}, bf16[256,256]{1,0:T(8,128)(2,1)S(1)}, u32[]{:S(2)}, u32[]{:S(2)}) collective-permute-start(bf16[256,256]{1,0:T(8,128)(2,1)S(1)} %collective-permute-done.9.refs_11_), channel_id=1, source_target_pairs={{0,1},{1,0},{2,3},{3,2},{4,5},{5,4},{6,7},{7,6},{8,9},{9,8},{10,11... | collective-permute-start | bytes 393224 | tf_op jit(solution)/shard_map/ppermute | solution.py:22
  23.2 6.5 %collective-permute-start.11 = (bf16[256,256]{1,0:T(8,128)(2,1)S(1)}, bf16[256,256]{1,0:T(8,128)(2,1)S(1)}, u32[]{:S(2)}, u32[]{:S(2)}) collective-permute-start(bf16[256,256]{1,0:T(8,128)(2,1)S(1)} %collective-permute-done.9.refs_11_), channel_id=1, source_target_pairs={{0,7},{1,2},{2,1},{3,4},{4,3},{5,6},{6,5},{7,0},{8,15},{9,10},{10,... | collective-permute-start | bytes 393224 | tf_op jit(solution)/shard_map/ppermute | solution.py:22
  25.8 5.0 %collective-permute-start.12 = (bf16[256,256]{1,0:T(8,128)(2,1)S(1)}, bf16[256,256]{1,0:T(8,128)(2,1)S(1)}, u32[]{:S(2)}, u32[]{:S(2)}) collective-permute-start(bf16[256,256]{1,0:T(8,128)(2,1)S(1)} %collective-permute-done.8.refs_10_), channel_id=1, source_target_pairs={{0,1},{1,0},{2,3},{3,2},{4,5},{5,4},{6,7},{7,6},{8,9},{9,8},{10,11... | collective-permute-start | bytes 393224 | tf_op jit(solution)/shard_map/ppermute | solution.py:22
  26.0 6.2 %collective-permute-start.13 = (bf16[256,256]{1,0:T(8,128)(2,1)S(1)}, bf16[256,256]{1,0:T(8,128)(2,1)S(1)}, u32[]{:S(2)}, u32[]{:S(2)}) collective-permute-start(bf16[256,256]{1,0:T(8,128)(2,1)S(1)} %collective-permute-done.7.refs_9_), channel_id=1, source_target_pairs={{0,7},{1,2},{2,1},{3,4},{4,3},{5,6},{6,5},{7,0},{8,15},{9,10},{10,... | collective-permute-start | bytes 393224 | tf_op jit(solution)/shard_map/ppermute | solution.py:22
  32.2 6.4 %copy-start.9 = (bf16[1,1024,1024]{2,1,0:T(8,128)(2,1)S(1)}, bf16[1,1024,1024]{2,1,0:T(8,128)(2,1)}, u32[]{:S(2)}) copy-start(bf16[1,1024,1024]{2,1,0:T(8,128)(2,1)} %param.23) | copy-start | bytes 6291460
  32.2 6.4 %copy-start.10 = (bf16[1,1024,1024]{2,1,0:T(8,128)(2,1)S(1)}, bf16[1,1024,1024]{2,1,0:T(8,128)(2,1)}, u32[]{:S(2)}) copy-start(bf16[1,1024,1024]{2,1,0:T(8,128)(2,1)} %param.21) | copy-start | bytes 6291460
  33.8 8.5 %collective-permute-start.14 = (bf16[2,2,64,256]{3,2,1,0:T(8,128)(2,1)S(1)}, bf16[2,2,64,256]{3,2,1,0:T(8,128)(2,1)S(1)}, u32[]{:S(2)}, u32[]{:S(2)}) collective-permute-start(bf16[2,2,64,256]{3,2,1,0:T(8,128)(2,1)S(1)} %get-tuple-element.11), channel_id=1, source_target_pairs={{0,64},{64,0},{128,192},{192,128},{1,65},{65,1},{129,193},{193,129... | collective-permute-start | bytes 393224 | tf_op jit(solution)/shard_map/ppermute | solution.py:22
  35.5 7.5 %collective-permute-start.15 = (bf16[2,2,64,256]{3,2,1,0:T(8,128)(2,1)S(1)}, bf16[2,2,64,256]{3,2,1,0:T(8,128)(2,1)S(1)}, u32[]{:S(2)}, u32[]{:S(2)}) collective-permute-start(bf16[2,2,64,256]{3,2,1,0:T(8,128)(2,1)S(1)} %get-tuple-element.12), channel_id=1, source_target_pairs={{0,128},{64,192},{128,0},{192,64},{1,129},{65,193},{129,1},{193,65... | collective-permute-start | bytes 393224 | tf_op jit(solution)/shard_map/ppermute | solution.py:22
  38.4 6.2 %copy-start.4 = (f32[2,2,64,256]{3,2,1,0:T(8,128)S(1)}, f32[2,2,64,256]{3,2,1,0:T(8,128)}, u32[]{:S(2)}) copy-start(f32[2,2,64,256]{3,2,1,0:T(8,128)} %param.20) | copy-start | bytes 786436
  38.4 6.2 %collective-permute-start.16 = (bf16[2,2,64,256]{3,2,1,0:T(8,128)(2,1)S(1)}, bf16[2,2,64,256]{3,2,1,0:T(8,128)(2,1)S(1)}, u32[]{:S(2)}, u32[]{:S(2)}) collective-permute-start(bf16[2,2,64,256]{3,2,1,0:T(8,128)(2,1)S(1)} %get-tuple-element.13), channel_id=1, source_target_pairs={{0,192},{64,128},{128,64},{192,0},{1,193},{65,129},{129,65},{193,1... | collective-permute-start | bytes 393224 | tf_op jit(solution)/shard_map/ppermute | solution.py:22
where the time goes:
time: 45.4 us; the launch traced here: 45.3 us
  starting transfers between devices  22.4 us (49%)
  waiting for transfers between devices  12.7 us (28%)
  matrix products  3.68 us (8%)
  Pallas kernels  3.57 us (8%)
  local copies, waits for them, and re-layouts  1.41 us (3%)
  other arithmetic  0.84 us (2%)
  between operations  0.75 us (2%)
    ppermute x17, starting transfers between devices, swap_with(): return lax.ppermute(x, axis, [(i, partner(i) % size) for i in range(size)])  22.4 us
    ppermute x17, waiting for transfers between devices, swap_with(): return lax.ppermute(x, axis, [(i, partner(i) % size) for i in range(size)])  12.7 us
    dot_general x1, matrix products, program(): update = jnp.dot(leaf_lower[0], leaf_upper[0], preferred_element_type=f32)  3.68 us
    pallas_call x2, Pallas kernels, call(): pl.pallas_call(body, out_shape=outs, in_specs=ins, out_specs=out_specs or...  3.57 us
    unnamed x23, local copies, waits for them, and re-layouts  1.34 us
  transfers between devices with their start and end apart: 17, of which 7 were waited for; matrix products, arithmetic and copies ran while one was open for 11% of the time, Pallas kernels for 4%

commit v1 on v0

--- a/solution.py
+++ b/solution.py
@@ -26,12 +26,13 @@
     return i + 1 if i % 2 else i - 1
 
 
-def call(body, outs, ins, args, flops, moved, scratch=(), out_specs=None):
+def call(body, outs, ins, args, flops, moved, scratch=(), aliases=None):
     return pl.pallas_call(
         body,
         out_shape=outs,
         in_specs=ins,
-        out_specs=out_specs or jax.tree.map(lambda _: VMEM, outs),
+        out_specs=jax.tree.map(lambda _: VMEM, outs),
+        input_output_aliases=aliases or {},
         scratch_shapes=list(scratch),
         cost_estimate=pl.CostEstimate(flops=flops, bytes_accessed=moved, transcendentals=0),
         compiler_params=pltpu.CompilerParams(vmem_limit_bytes=VMEM_LIMIT),
@@ -62,21 +63,21 @@
     acc[p] += jnp.dot(low, up[k], preferred_element_type=jnp.float32)
 
 
-def near_body(meta, inv, *refs):
-    uppers, lowers, (up, acc) = refs[: len(U_FLIPS)], refs[len(U_FLIPS) : -2], refs[-2:]
+def early_body(meta, inv, *refs):
+    up = refs[-1]
     up[...] = jnp.zeros_like(up)
+    for n, ref in enumerate(refs[:-1]):
+        add_upper(ref[...], n, meta, inv, up)
+
+
+def near_body(meta, inv, up_in, *refs):
+    half = len(U_FLIPS) // 2
+    uppers, lowers, (up, acc) = refs[:half], refs[half:-2], refs[-2:]
     acc[...] = jnp.zeros_like(acc)
     for n, ref in enumerate(uppers):
-        add_upper(ref[...], n, meta, inv, up)
+        add_upper(ref[...], half + n, meta, inv, up)
     for n, ref in enumerate(lowers):
         add_lower(ref[...], n, meta, inv, up, acc)
-
-
-def mid_body(meta, inv, up, acc_in, *refs, first):
-    acc = refs[-1]
-    acc[...] = acc_in[...]
-    for n, ref in enumerate(refs[:-1]):
-        add_lower(ref[...], first + n, meta, inv, up, acc)
 
 
 def far_body(meta, inv, up, acc_in, *refs, first):
@@ -129,31 +130,32 @@
     fo = swap_with(be, "col", cols, other_pair)
     ge = swap_with(b4, "col", cols, lambda i: i ^ 1)
     go = swap_with(b4, "col", cols, other_pair)
-    near, mid, far = (b, be, bo, b4), (), (ge, go, fe, fo)
+    near, far = (b, be, bo, b4), (ge, go, fe, fo)
     theirs = tuple(swap_with(x, "row", rows, lambda i: i ^ 1) for x in ours)
     meta = jnp.concatenate([u_ids, l_ids, col_order[None], row_order[None]], axis=1)
     invs = jnp.concatenate([inv_lower, inv_upper])
 
+    panel = sds((panels, tile, 2 * tile), bf)
+    up = call(
+        early_body,
+        panel,
+        [SMEM] + [VMEM] * (1 + len(ours)),
+        (meta, invs, *ours),
+        flops=2 * 4 * tile**3,
+        moved=4 << 20,
+    )
     up, acc = call(
         near_body,
-        (sds((panels, tile, 2 * tile), bf), sds((2, tile, 2 * tile), f32)),
-        [SMEM] + [VMEM] * (1 + 8 + len(near)),
-        (meta, invs, *ours, *theirs, *near),
-        flops=2 * (8 + 3 * len(near)) * tile**3,
+        (panel, sds((2, tile, 2 * tile), f32)),
+        [SMEM] + [VMEM] * (2 + len(theirs) + len(near)),
+        (meta, invs, up, *theirs, *near),
+        flops=2 * (4 + 3 * len(near)) * tile**3,
         moved=4 << 20,
+        aliases={2: 0},
     )
-    if mid:
-        acc = call(
-            functools.partial(mid_body, first=len(near)),
-            sds((2, tile, 2 * tile), f32),
-            [SMEM] + [VMEM] * (3 + len(mid)),
-            (meta, invs, up, acc, *mid),
-            flops=2 * 3 * len(mid) * tile**3,
-            moved=4 << 20,
-        )
     piece = (2, 2, part, tile)
     s1, s2, s3, own = call(
-        functools.partial(far_body, first=len(near) + len(mid)),
+        functools.partial(far_body, first=len(near)),
         (sds(piece, bf), sds(piece, bf), sds(piece, bf), sds(piece, f32)),
         [SMEM] + [VMEM] * (3 + len(far)),
         (meta, invs, up, acc, *far),

time: 45.4 us -> 45.4 us (level)
  waiting for transfers between devices: 12.7 us -> 12 us
  Pallas kernels: 3.57 us -> 4.25 us
    ppermute x17, waiting for transfers between devices: 12.7 us -> 12 us  [swap_with(): return lax.ppermute(x, axis, [(i, partner(i) % size) for i in range(size)])]
    pallas_call x2 -> x3, Pallas kernels: 3.57 us -> 4.25 us  [call(): pl.pallas_call(body, out_shape=outs, in_specs=ins, out_specs=jax.tree.map...]
  transfers between devices with their start and end apart: 17 -> 17, of which waited for: 7 -> 6; matrix products, arithmetic and copies ran while one was open for 11% -> 11% of each run, Pallas kernels for 4% -> 6%
where the time goes in v1:
time: 45.4 us; the launch traced here: 45.3 us
  starting transfers between devices  22.4 us (49%)
  waiting for transfers between devices  12 us (26%)
  Pallas kernels  4.25 us (9%)
  matrix products  3.68 us (8%)
  local copies, waits for them, and re-layouts  1.41 us (3%)
  other arithmetic  0.84 us (2%)
  between operations  0.77 us (2%)
    ppermute x17, starting transfers between devices, swap_with(): return lax.ppermute(x, axis, [(i, partner(i) % size) for i in range(size)])  22.4 us
    ppermute x17, waiting for transfers between devices, swap_with(): return lax.ppermute(x, axis, [(i, partner(i) % size) for i in range(size)])  12 us
    pallas_call x3, Pallas kernels, call(): pl.pallas_call(body, out_shape=outs, in_specs=ins, out_specs=jax.tree.map...  4.25 us
    dot_general x1, matrix products, program(): update = jnp.dot(leaf_lower[0], leaf_upper[0], preferred_element_type=f32)  3.68 us
    unnamed x23, local copies, waits for them, and re-layouts  1.34 us
  transfers between devices with their start and end apart: 17, of which 6 were waited for; matrix products, arithmetic and copies ran while one was open for 11% of the time, Pallas kernels for 6%

profile of v1, /device:TPU:2, one launch (start us, length us, event | category | flops | bytes accessed | tf_op | source)
XLA Modules:
  0.0 45.3 jit_solution(16098083088343263868)
XLA Ops:
  0.6 0.0 copy-start
  0.6 0.0 copy-start.2
  0.7 0.0 copy-start.3
  0.7 2.3 %collective-permute-start = (bf16[256,256]{1,0:T(8,128)(2,1)}, bf16[256,256]{1,0:T(8,128)(2,1)S(1)}, u32[]{:S(2)}, u32[]{:S(2)}) collective-permute-start(bf16[256,256]{1,0:T(8,128)(2,1)} %bitcast.19), channel_id=1, source_target_pairs={{0,16},{8,24},{16,0},{24,8},{32,48},{40,56},{48,32},{56,40},{1,17}... | collective-permute-start | bytes 393224 | tf_op jit(solution)/shard_map/ppermute | solution.py:22
  3.0 0.4 collective-permute-start.1
  3.4 1.7 %collective-permute-start.2 = (bf16[256,256]{1,0:T(8,128)(2,1)}, bf16[256,256]{1,0:T(8,128)(2,1)S(1)}, u32[]{:S(2)}, u32[]{:S(2)}) collective-permute-start(bf16[256,256]{1,0:T(8,128)(2,1)} %bitcast.21), channel_id=1, source_target_pairs={{0,32},{8,40},{16,48},{24,56},{32,0},{40,8},{48,16},{56,24},{1,33}... | collective-permute-start | bytes 393224 | tf_op jit(solution)/shard_map/ppermute | solution.py:22
  5.2 0.0 collective-permute-start.3
  5.2 0.0 copy-start.5
  5.2 0.0 copy-start.6
  5.2 0.0 copy-start.7
  5.2 0.0 copy-start.8
  5.2 0.0 copy-start.1
  5.2 7.0 %collective-permute-start.9 = (bf16[256,256]{1,0:T(8,128)(2,1)}, bf16[256,256]{1,0:T(8,128)(2,1)S(1)}, u32[]{:S(2)}, u32[]{:S(2)}) collective-permute-start(bf16[256,256]{1,0:T(8,128)(2,1)} %bitcast.24), channel_id=1, source_target_pairs={{0,4},{1,5},{2,6},{3,7},{4,0},{5,1},{6,2},{7,3},{8,12},{9,13},{10,... | collective-permute-start | bytes 393224 | tf_op jit(solution)/shard_map/ppermute | solution.py:22
  12.2 1.3 %constant_dynamic-update-slice_fusion.1 = bf16[16,256,256]{2,1,0:T(8,128)(2,1)S(1)} fusion(bf16[8,256,256]{2,1,0:T(8,128)(2,1)} %param.17), kind=kLoop, calls=%fused_computation.8 | loop fusion | bytes 2097152
  13.5 0.0 collective-permute-done.refs_1_
  13.5 0.0 copy-done.2
  13.5 1.1 %collective-permute-start.7 = (bf16[256,256]{1,0:T(8,128)(2,1)S(1)}, bf16[256,256]{1,0:T(8,128)(2,1)S(1)}, u32[]{:S(2)}, u32[]{:S(2)}) collective-permute-start(bf16[256,256]{1,0:T(8,128)(2,1)S(1)} %bitcast.25), channel_id=1, source_target_pairs={{0,1},{1,0},{2,3},{3,2},{4,5},{5,4},{6,7},{7,6},{8,9},{9,8},{10,11... | collective-permute-start | bytes 393224 | tf_op jit(solution)/shard_map/ppermute | solution.py:22
  14.6 0.0 collective-permute-done.1.refs_2_
  14.6 0.3 collective-permute-start.8
  14.9 0.0 collective-permute-done.2.refs_3_
  14.9 0.0 collective-permute-start.4
  14.9 3.2 %collective-permute-done.9.refs_7_ = bf16[256,256]{1,0:T(8,128)(2,1)S(1)} collective-permute-done((bf16[256,256]{1,0:T(8,128)(2,1)}, bf16[256,256]{1,0:T(8,128)(2,1)S(1)}, u32[]{:S(2)}, u32[]{:S(2)}) %collective-permute-start.9) | collective-permute-done | bytes 131104 | tf_op jit(solution)/shard_map/ppermute | solution.py:22
  18.1 0.0 collective-permute-start.5
  18.1 0.0 collective-permute-done.3.refs_0_
  18.1 0.5 %collective-permute-start.6 = (bf16[256,256]{1,0:T(8,128)(2,1)S(1)}, bf16[256,256]{1,0:T(8,128)(2,1)S(1)}, u32[]{:S(2)}, u32[]{:S(2)}) collective-permute-start(bf16[256,256]{1,0:T(8,128)(2,1)S(1)} %collective-permute-done.2.refs_3_), channel_id=1, source_target_pairs={{0,8},{8,0},{16,24},{24,16},{32,40},{40,32},{48,56},{56,48},{1,9},... | collective-permute-start | bytes 393224 | tf_op jit(solution)/shard_map/ppermute | solution.py:22
  18.6 0.0 copy-done.3
  18.6 0.1 constant_dynamic-update-slice_fusion.inv
  18.7 4.2 %collective-permute-done.7.refs_5_ = bf16[256,256]{1,0:T(8,128)(2,1)S(1)} collective-permute-done((bf16[256,256]{1,0:T(8,128)(2,1)S(1)}, bf16[256,256]{1,0:T(8,128)(2,1)S(1)}, u32[]{:S(2)}, u32[]{:S(2)}) %collective-permute-start.7) | collective-permute-done | bytes 131104 | tf_op jit(solution)/shard_map/ppermute | solution.py:22
  22.9 0.2 collective-permute-start.10
  23.2 0.0 collective-permute-done.8.refs_6_
  23.2 2.6 %collective-permute-start.11 = (bf16[256,256]{1,0:T(8,128)(2,1)S(1)}, bf16[256,256]{1,0:T(8,128)(2,1)S(1)}, u32[]{:S(2)}, u32[]{:S(2)}) collective-permute-start(bf16[256,256]{1,0:T(8,128)(2,1)S(1)} %collective-permute-done.9.refs_7_), channel_id=1, source_target_pairs={{0,7},{1,2},{2,1},{3,4},{4,3},{5,6},{6,5},{7,0},{8,15},{9,10},{10,... | collective-permute-start | bytes 393224 | tf_op jit(solution)/shard_map/ppermute | solution.py:22
  25.8 0.0 collective-permute-done.4.refs_1_
  25.8 0.2 collective-permute-start.12
  26.0 0.0 collective-permute-done.5.refs_2_
  26.0 1.1 %collective-permute-start.13 = (bf16[256,256]{1,0:T(8,128)(2,1)S(1)}, bf16[256,256]{1,0:T(8,128)(2,1)S(1)}, u32[]{:S(2)}, u32[]{:S(2)}) collective-permute-start(bf16[256,256]{1,0:T(8,128)(2,1)S(1)} %collective-permute-done.7.refs_5_), channel_id=1, source_target_pairs={{0,7},{1,2},{2,1},{3,4},{4,3},{5,6},{6,5},{7,0},{8,15},{9,10},{10,... | collective-permute-start | bytes 393224 | tf_op jit(solution)/shard_map/ppermute | solution.py:22
  27.1 0.0 copy-done.5
  27.1 0.0 copy-done.6
  27.1 0.0 copy-done.7
  27.1 0.0 copy-done.8
  27.1 0.1 pad_add_fusion.meta
  27.2 0.0 copy-done.1
  27.2 0.9 %shard_map.131.up_in = bf16[8,256,512]{2,1,0:T(8,128)(2,1)S(1)} custom-call(s32[1,160]{1,0:T(1,128)S(1)} %pad_add_fusion.meta, bf16[16,256,256]{2,1,0:T(8,128)(2,1)S(1)} %constant_dynamic-update-slice_fusion.inv, bf16[256,256]{1,0:T(8,128)(2,1)S(1)} %bitcast.23, bf16[256,256]{1,0:T(8,128)(2,1)S(1)} %collective-permute-done.refs_1_, ...), custom_call_target="tpu_custom_call" | custom-call | flops 134217728 | bytes 4194304 | tf_op jit(solution)/shard_map/pallas_call | solution.py:30
  28.1 0.0 collective-permute-done.6.refs_3_
  28.1 1.7 %shard_map.132 = (bf16[8,256,512]{2,1,0:T(8,128)(2,1)S(1)}, f32[2,256,512]{2,1,0:T(8,128)S(1)}) custom-call(s32[1,160]{1,0:T(1,128)S(1)} %pad_add_fusion.meta, bf16[16,256,256]{2,1,0:T(8,128)(2,1)S(1)} %constant_dynamic-update-slice_fusion.inv, bf16[8,256,512]{2,1,0:T(8,128)(2,1)S(1)} %shard_map.131.up_in, ...), custom_call_target="tpu_custom_call", output_to_operand_aliasing={{0}: (2, {})} | custom-call | flops 536870912 | bytes 4194304 | tf_op jit(solution)/shard_map/pallas_call | solution.py:30
  29.9 0.0 collective-permute-done.10.refs_0_
  29.9 0.0 collective-permute-done.11.refs_1_
  29.9 0.9 %collective-permute-done.12.refs_2_ = bf16[256,256]{1,0:T(8,128)(2,1)S(1)} collective-permute-done((bf16[256,256]{1,0:T(8,128)(2,1)S(1)}, bf16[256,256]{1,0:T(8,128)(2,1)S(1)}, u32[]{:S(2)}, u32[]{:S(2)}) %collective-permute-start.12) | collective-permute-done | bytes 131104 | tf_op jit(solution)/shard_map/ppermute | solution.py:22
  30.8 1.4 %collective-permute-done.13.refs_3_ = bf16[256,256]{1,0:T(8,128)(2,1)S(1)} collective-permute-done((bf16[256,256]{1,0:T(8,128)(2,1)S(1)}, bf16[256,256]{1,0:T(8,128)(2,1)S(1)}, u32[]{:S(2)}, u32[]{:S(2)}) %collective-permute-start.13) | collective-permute-done | bytes 131104 | tf_op jit(solution)/shard_map/ppermute | solution.py:22
  32.2 0.0 copy-start.9
  32.2 0.0 copy-start.10
  32.2 1.6 %shard_map.133 = (bf16[2,2,64,256]{3,2,1,0:T(8,128)(2,1)S(1)}, bf16[2,2,64,256]{3,2,1,0:T(8,128)(2,1)S(1)}, bf16[2,2,64,256]{3,2,1,0:T(8,128)(2,1)S(1)}, f32[2,2,64,256]{3,2,1,0:T(8,128)S(1)}) custom-call(s32[1,160]{1,0:T(1,128)S(1)} %pad_add_fusion.meta, bf16[16,256,256]{2,1,0:T(8,128)(2,1)S(1)} %constant_dynamic-update-slice_fusion.inv, ...), custom_call_target="tpu_custom_call" | custom-call | flops 402653184 | bytes 4194304 | tf_op jit(solution)/shard_map/pallas_call | solution.py:30
  33.8 1.7 %collective-permute-start.14 = (bf16[2,2,64,256]{3,2,1,0:T(8,128)(2,1)S(1)}, bf16[2,2,64,256]{3,2,1,0:T(8,128)(2,1)S(1)}, u32[]{:S(2)}, u32[]{:S(2)}) collective-permute-start(bf16[2,2,64,256]{3,2,1,0:T(8,128)(2,1)S(1)} %get-tuple-element.11), channel_id=1, source_target_pairs={{0,64},{64,0},{128,192},{192,128},{1,65},{65,1},{129,193},{193,129... | collective-permute-start | bytes 393224 | tf_op jit(solution)/shard_map/ppermute | solution.py:22
  35.5 2.9 %collective-permute-start.15 = (bf16[2,2,64,256]{3,2,1,0:T(8,128)(2,1)S(1)}, bf16[2,2,64,256]{3,2,1,0:T(8,128)(2,1)S(1)}, u32[]{:S(2)}, u32[]{:S(2)}) collective-permute-start(bf16[2,2,64,256]{3,2,1,0:T(8,128)(2,1)S(1)} %get-tuple-element.12), channel_id=1, source_target_pairs={{0,128},{64,192},{128,0},{192,64},{1,129},{65,193},{129,1},{193,65... | collective-permute-start | bytes 393224 | tf_op jit(solution)/shard_map/ppermute | solution.py:22
  38.4 0.0 copy-start.4
  38.4 0.2 collective-permute-start.16
  38.6 0.0 copy-done
  38.6 0.0 copy-done.9
  38.6 0.0 copy-done.10
  38.6 3.7 %fusion.1 = bf16[1,1024,1024]{2,1,0:T(8,128)(2,1)} fusion(bf16[1,1024,1024]{2,1,0:T(8,128)(2,1)S(1)} %copy-done.9, bf16[1,1024,1024]{2,1,0:T(8,128)(2,1)S(1)} %copy-done, bf16[1,1024,1024]{2,1,0:T(8,128)(2,1)S(1)} %copy-done.10), kind=kOutput, calls=%fused_computation.2 | convolution fusion | flops 2150629376 | bytes 8388608 | tf_op jit(solution)/shard_map/dot_general | solution.py:171
  42.3 0.0 collective-permute-done.14
  42.3 0.7 %collective-permute-done.15 = bf16[2,2,64,256]{3,2,1,0:T(8,128)(2,1)S(1)} collective-permute-done((bf16[2,2,64,256]{3,2,1,0:T(8,128)(2,1)S(1)}, bf16[2,2,64,256]{3,2,1,0:T(8,128)(2,1)S(1)}, u32[]{:S(2)}, u32[]{:S(2)}) %collective-permute-start.15) | collective-permute-done | bytes 131104 | tf_op jit(solution)/shard_map/ppermute | solution.py:22
  43.0 1.5 %collective-permute-done.16 = bf16[2,2,64,256]{3,2,1,0:T(8,128)(2,1)S(1)} collective-permute-done((bf16[2,2,64,256]{3,2,1,0:T(8,128)(2,1)S(1)}, bf16[2,2,64,256]{3,2,1,0:T(8,128)(2,1)S(1)}, u32[]{:S(2)}, u32[]{:S(2)}) %collective-permute-start.16) | collective-permute-done | bytes 131104 | tf_op jit(solution)/shard_map/ppermute | solution.py:22
  44.5 0.0 copy-done.4
  44.5 0.8 %add_subtract_fusion = f32[2,2,64,256]{3,2,1,0:T(8,128)} fusion(f32[2,2,64,256]{3,2,1,0:T(8,128)S(1)} %copy-done.4, bf16[2,2,64,256]{3,2,1,0:T(8,128)(2,1)S(1)} %collective-permute-done.16, bf16[2,2,64,256]{3,2,1,0:T(8,128)(2,1)S(1)} %collective-permute-done.15, f32[2,2,64,256]{3,2,1,0:T(8,128)S(1)} %get-tuple-element.10, ...), kind=kLoop, calls=%fused_computation.6 | loop fusion | flops 458752 | bytes 1179648 | tf_op jit(solution)/shard_map/sub | solution.py:169
Async XLA Ops:
  0.6 38.0 %copy-start = (bf16[1,1024,1024]{2,1,0:T(8,128)(2,1)S(1)}, bf16[1,1024,1024]{2,1,0:T(8,128)(2,1)}, u32[]{:S(2)}) copy-start(bf16[1,1024,1024]{2,1,0:T(8,128)(2,1)} %param.22) | copy-start | bytes 6291460
  0.6 12.8 %copy-start.2 = (bf16[1,1,256,256]{3,2,1,0:T(8,128)(2,1)S(1)}, bf16[1,1,256,256]{3,2,1,0:T(8,128)(2,1)}, u32[]{:S(2)}) copy-start(bf16[1,1,256,256]{3,2,1,0:T(8,128)(2,1)} %param.12) | copy-start | bytes 393220
  0.7 18.0 %copy-start.3 = (bf16[8,256,256]{2,1,0:T(8,128)(2,1)S(1)}, bf16[8,256,256]{2,1,0:T(8,128)(2,1)}, u32[]{:S(2)}) copy-start(bf16[8,256,256]{2,1,0:T(8,128)(2,1)} %param.16) | copy-start | bytes 3145732
  0.7 12.8 %collective-permute-start = (bf16[256,256]{1,0:T(8,128)(2,1)}, bf16[256,256]{1,0:T(8,128)(2,1)S(1)}, u32[]{:S(2)}, u32[]{:S(2)}) collective-permute-start(bf16[256,256]{1,0:T(8,128)(2,1)} %bitcast.19), channel_id=1, source_target_pairs={{0,16},{8,24},{16,0},{24,8},{32,48},{40,56},{48,32},{56,40},{1,17}... | collective-permute-start | bytes 393224 | tf_op jit(solution)/shard_map/ppermute | solution.py:22
  3.0 11.6 %collective-permute-start.1 = (bf16[256,256]{1,0:T(8,128)(2,1)}, bf16[256,256]{1,0:T(8,128)(2,1)S(1)}, u32[]{:S(2)}, u32[]{:S(2)}) collective-permute-start(bf16[256,256]{1,0:T(8,128)(2,1)} %bitcast.20), channel_id=1, source_target_pairs={{0,48},{8,56},{16,32},{24,40},{32,16},{40,24},{48,0},{56,8},{1,49}... | collective-permute-start | bytes 393224 | tf_op jit(solution)/shard_map/ppermute | solution.py:22
  3.4 11.5 %collective-permute-start.2 = (bf16[256,256]{1,0:T(8,128)(2,1)}, bf16[256,256]{1,0:T(8,128)(2,1)S(1)}, u32[]{:S(2)}, u32[]{:S(2)}) collective-permute-start(bf16[256,256]{1,0:T(8,128)(2,1)} %bitcast.21), channel_id=1, source_target_pairs={{0,32},{8,40},{16,48},{24,56},{32,0},{40,8},{48,16},{56,24},{1,33}... | collective-permute-start | bytes 393224 | tf_op jit(solution)/shard_map/ppermute | solution.py:22
  5.2 12.9 %collective-permute-start.3 = (bf16[256,256]{1,0:T(8,128)(2,1)}, bf16[256,256]{1,0:T(8,128)(2,1)S(1)}, u32[]{:S(2)}, u32[]{:S(2)}) collective-permute-start(bf16[256,256]{1,0:T(8,128)(2,1)} %bitcast.22), channel_id=1, source_target_pairs={{0,8},{8,0},{16,24},{24,16},{32,40},{40,32},{48,56},{56,48},{1,9},... | collective-permute-start | bytes 393224 | tf_op jit(solution)/shard_map/ppermute | solution.py:22
  5.2 21.9 %copy-start.5 = (s32[16]{0:T(128)S(1)}, s32[16]{0:T(128)}, u32[]{:S(2)}) copy-start(s32[16]{0:T(128)} %param.18) | copy-start | bytes 196
  5.2 21.9 %copy-start.6 = (s32[16]{0:T(128)S(1)}, s32[16]{0:T(128)}, u32[]{:S(2)}) copy-start(s32[16]{0:T(128)} %param.19) | copy-start | bytes 196
  5.2 21.9 %copy-start.7 = (s32[1,64]{1,0:T(1,128)S(1)}, s32[1,64]{1,0:T(1,128)}, u32[]{:S(2)}) copy-start(s32[1,64]{1,0:T(1,128)} %param.13) | copy-start | bytes 772
  5.2 21.9 %copy-start.8 = (s32[1,64]{1,0:T(1,128)S(1)}, s32[1,64]{1,0:T(1,128)}, u32[]{:S(2)}) copy-start(s32[1,64]{1,0:T(1,128)} %param.15) | copy-start | bytes 772
  5.2 22.0 %copy-start.1 = (bf16[1,1,256,256]{3,2,1,0:T(8,128)(2,1)S(1)}, bf16[1,1,256,256]{3,2,1,0:T(8,128)(2,1)}, u32[]{:S(2)}) copy-start(bf16[1,1,256,256]{3,2,1,0:T(8,128)(2,1)} %param.14) | copy-start | bytes 393220
  5.2 12.9 %collective-permute-start.9 = (bf16[256,256]{1,0:T(8,128)(2,1)}, bf16[256,256]{1,0:T(8,128)(2,1)S(1)}, u32[]{:S(2)}, u32[]{:S(2)}) collective-permute-start(bf16[256,256]{1,0:T(8,128)(2,1)} %bitcast.24), channel_id=1, source_target_pairs={{0,4},{1,5},{2,6},{3,7},{4,0},{5,1},{6,2},{7,3},{8,12},{9,13},{10,... | collective-permute-start | bytes 393224 | tf_op jit(solution)/shard_map/ppermute | solution.py:22
  13.5 9.4 %collective-permute-start.7 = (bf16[256,256]{1,0:T(8,128)(2,1)S(1)}, bf16[256,256]{1,0:T(8,128)(2,1)S(1)}, u32[]{:S(2)}, u32[]{:S(2)}) collective-permute-start(bf16[256,256]{1,0:T(8,128)(2,1)S(1)} %bitcast.25), channel_id=1, source_target_pairs={{0,1},{1,0},{2,3},{3,2},{4,5},{5,4},{6,7},{7,6},{8,9},{9,8},{10,11... | collective-permute-start | bytes 393224 | tf_op jit(solution)/shard_map/ppermute | solution.py:22
  14.6 8.6 %collective-permute-start.8 = (bf16[256,256]{1,0:T(8,128)(2,1)S(1)}, bf16[256,256]{1,0:T(8,128)(2,1)S(1)}, u32[]{:S(2)}, u32[]{:S(2)}) collective-permute-start(bf16[256,256]{1,0:T(8,128)(2,1)S(1)} %bitcast.26), channel_id=1, source_target_pairs={{0,7},{1,2},{2,1},{3,4},{4,3},{5,6},{6,5},{7,0},{8,15},{9,10},{10,... | collective-permute-start | bytes 393224 | tf_op jit(solution)/shard_map/ppermute | solution.py:22
  14.9 10.9 %collective-permute-start.4 = (bf16[256,256]{1,0:T(8,128)(2,1)S(1)}, bf16[256,256]{1,0:T(8,128)(2,1)S(1)}, u32[]{:S(2)}, u32[]{:S(2)}) collective-permute-start(bf16[256,256]{1,0:T(8,128)(2,1)S(1)} %collective-permute-done.refs_1_), channel_id=1, source_target_pairs={{0,8},{8,0},{16,24},{24,16},{32,40},{40,32},{48,56},{56,48},{1,9},... | collective-permute-start | bytes 393224 | tf_op jit(solution)/shard_map/ppermute | solution.py:22
  18.1 7.9 %collective-permute-start.5 = (bf16[256,256]{1,0:T(8,128)(2,1)S(1)}, bf16[256,256]{1,0:T(8,128)(2,1)S(1)}, u32[]{:S(2)}, u32[]{:S(2)}) collective-permute-start(bf16[256,256]{1,0:T(8,128)(2,1)S(1)} %collective-permute-done.1.refs_2_), channel_id=1, source_target_pairs={{0,8},{8,0},{16,24},{24,16},{32,40},{40,32},{48,56},{56,48},{1,9},... | collective-permute-start | bytes 393224 | tf_op jit(solution)/shard_map/ppermute | solution.py:22
  18.1 10.0 %collective-permute-start.6 = (bf16[256,256]{1,0:T(8,128)(2,1)S(1)}, bf16[256,256]{1,0:T(8,128)(2,1)S(1)}, u32[]{:S(2)}, u32[]{:S(2)}) collective-permute-start(bf16[256,256]{1,0:T(8,128)(2,1)S(1)} %collective-permute-done.2.refs_3_), channel_id=1, source_target_pairs={{0,8},{8,0},{16,24},{24,16},{32,40},{40,32},{48,56},{56,48},{1,9},... | collective-permute-start | bytes 393224 | tf_op jit(solution)/shard_map/ppermute | solution.py:22
  22.9 6.9 %collective-permute-start.10 = (bf16[256,256]{1,0:T(8,128)(2,1)S(1)}, bf16[256,256]{1,0:T(8,128)(2,1)S(1)}, u32[]{:S(2)}, u32[]{:S(2)}) collective-permute-start(bf16[256,256]{1,0:T(8,128)(2,1)S(1)} %collective-permute-done.9.refs_7_), channel_id=1, source_target_pairs={{0,1},{1,0},{2,3},{3,2},{4,5},{5,4},{6,7},{7,6},{8,9},{9,8},{10,11... | collective-permute-start | bytes 393224 | tf_op jit(solution)/shard_map/ppermute | solution.py:22
  23.2 6.7 %collective-permute-start.11 = (bf16[256,256]{1,0:T(8,128)(2,1)S(1)}, bf16[256,256]{1,0:T(8,128)(2,1)S(1)}, u32[]{:S(2)}, u32[]{:S(2)}) collective-permute-start(bf16[256,256]{1,0:T(8,128)(2,1)S(1)} %collective-permute-done.9.refs_7_), channel_id=1, source_target_pairs={{0,7},{1,2},{2,1},{3,4},{4,3},{5,6},{6,5},{7,0},{8,15},{9,10},{10,... | collective-permute-start | bytes 393224 | tf_op jit(solution)/shard_map/ppermute | solution.py:22
  25.8 5.0 %collective-permute-start.12 = (bf16[256,256]{1,0:T(8,128)(2,1)S(1)}, bf16[256,256]{1,0:T(8,128)(2,1)S(1)}, u32[]{:S(2)}, u32[]{:S(2)}) collective-permute-start(bf16[256,256]{1,0:T(8,128)(2,1)S(1)} %collective-permute-done.8.refs_6_), channel_id=1, source_target_pairs={{0,1},{1,0},{2,3},{3,2},{4,5},{5,4},{6,7},{7,6},{8,9},{9,8},{10,11... | collective-permute-start | bytes 393224 | tf_op jit(solution)/shard_map/ppermute | solution.py:22
  26.0 6.2 %collective-permute-start.13 = (bf16[256,256]{1,0:T(8,128)(2,1)S(1)}, bf16[256,256]{1,0:T(8,128)(2,1)S(1)}, u32[]{:S(2)}, u32[]{:S(2)}) collective-permute-start(bf16[256,256]{1,0:T(8,128)(2,1)S(1)} %collective-permute-done.7.refs_5_), channel_id=1, source_target_pairs={{0,7},{1,2},{2,1},{3,4},{4,3},{5,6},{6,5},{7,0},{8,15},{9,10},{10,... | collective-permute-start | bytes 393224 | tf_op jit(solution)/shard_map/ppermute | solution.py:22
  32.2 6.4 %copy-start.9 = (bf16[1,1024,1024]{2,1,0:T(8,128)(2,1)S(1)}, bf16[1,1024,1024]{2,1,0:T(8,128)(2,1)}, u32[]{:S(2)}) copy-start(bf16[1,1024,1024]{2,1,0:T(8,128)(2,1)} %param.23) | copy-start | bytes 6291460
  32.2 6.4 %copy-start.10 = (bf16[1,1024,1024]{2,1,0:T(8,128)(2,1)S(1)}, bf16[1,1024,1024]{2,1,0:T(8,128)(2,1)}, u32[]{:S(2)}) copy-start(bf16[1,1024,1024]{2,1,0:T(8,128)(2,1)} %param.21) | copy-start | bytes 6291460
  33.8 8.5 %collective-permute-start.14 = (bf16[2,2,64,256]{3,2,1,0:T(8,128)(2,1)S(1)}, bf16[2,2,64,256]{3,2,1,0:T(8,128)(2,1)S(1)}, u32[]{:S(2)}, u32[]{:S(2)}) collective-permute-start(bf16[2,2,64,256]{3,2,1,0:T(8,128)(2,1)S(1)} %get-tuple-element.11), channel_id=1, source_target_pairs={{0,64},{64,0},{128,192},{192,128},{1,65},{65,1},{129,193},{193,129... | collective-permute-start | bytes 393224 | tf_op jit(solution)/shard_map/ppermute | solution.py:22
  35.5 7.5 %collective-permute-start.15 = (bf16[2,2,64,256]{3,2,1,0:T(8,128)(2,1)S(1)}, bf16[2,2,64,256]{3,2,1,0:T(8,128)(2,1)S(1)}, u32[]{:S(2)}, u32[]{:S(2)}) collective-permute-start(bf16[2,2,64,256]{3,2,1,0:T(8,128)(2,1)S(1)} %get-tuple-element.12), channel_id=1, source_target_pairs={{0,128},{64,192},{128,0},{192,64},{1,129},{65,193},{129,1},{193,65... | collective-permute-start | bytes 393224 | tf_op jit(solution)/shard_map/ppermute | solution.py:22
  38.4 6.2 %copy-start.4 = (f32[2,2,64,256]{3,2,1,0:T(8,128)S(1)}, f32[2,2,64,256]{3,2,1,0:T(8,128)}, u32[]{:S(2)}) copy-start(f32[2,2,64,256]{3,2,1,0:T(8,128)} %param.20) | copy-start | bytes 786436
  38.4 6.2 %collective-permute-start.16 = (bf16[2,2,64,256]{3,2,1,0:T(8,128)(2,1)S(1)}, bf16[2,2,64,256]{3,2,1,0:T(8,128)(2,1)S(1)}, u32[]{:S(2)}, u32[]{:S(2)}) collective-permute-start(bf16[2,2,64,256]{3,2,1,0:T(8,128)(2,1)S(1)} %get-tuple-element.13), channel_id=1, source_target_pairs={{0,192},{64,128},{128,64},{192,0},{1,193},{65,129},{129,65},{193,1... | collective-permute-start | bytes 393224 | tf_op jit(solution)/shard_map/ppermute | solution.py:22
